TPU v7x, 32 devices: a whole 2x2x4 slice. The times are simulated.
32 devices in a mesh: span: 16 (over z, y, x), wall: 2 (over core).
Axes of the slice: x: 2, y: 2, z: 4, core: 2. Of those that a mesh axis runs over, the one named last changes fastest.
Arguments:
- velocity: bfloat16 [64, 3, 8, 128, 256], P(None, None, None, 'span', 'wall'), may hold values from -1080 to 1080, as said below
- wall_metric: float32 [256], P('wall'), may hold values from 0.5 to 2
Outputs:
- modes: bfloat16 [64, 3, 2, 128, 256], P(None, None, None, 'span', 'wall')
- r_factor: float32 [64, 64], replicated
Inputs may be any that keep to these rules, and one draw needn't show every extreme that they name: velocity fields of order up to a few hundred.
All inputs are finite; a program needn't handle non-finite values.
Results may differ from a plain program's by a relative error of at most 0.0063.
Values may be sent and summed in bfloat16 or wider, within the bound.
A program may use at most 64 MiB of HBM per device.

v0:
```python
import jax
import jax.numpy as jnp
from jax import lax
from jax.sharding import PartitionSpec as P


def padded_2(block, sides, width, periodic):
    for axis, dim in sides:
        count = lax.axis_size(axis)
        forward = [(i, i + 1) for i in range(count - 1)]
        if periodic:
            forward.append((count - 1, 0))
        backward = [(target, source) for source, target in forward]
        low = lax.ppermute(
            lax.slice_in_dim(block, block.shape[dim] - width, None, axis=dim), axis, forward
        )
        high = lax.ppermute(lax.slice_in_dim(block, 0, width, axis=dim), axis, backward)
        block = jnp.concatenate([low, block, high], axis=dim)
    return block


def stencil(padded, axis, length):

    def take(k):
        return lax.slice_in_dim(padded, 3 + k, 3 + k + length, axis=axis).astype(jnp.float32)

    return (45.0 * (take(1) - take(-1)) - 9.0 * (take(2) - take(-2)) + (take(3) - take(-3))) / 60.0


def factor_lower(gram):
    order = gram.shape[0]
    positions = jnp.arange(order, dtype=jnp.int32)

    def column(index, lower):
        at = jnp.asarray(index).astype(jnp.int32)
        above = lax.dynamic_slice_in_dim(gram, at, 1, 1)[:, 0]
        row_j = lax.dynamic_slice_in_dim(lower, at, 1, 0)[0]
        rest = above - jnp.sum(lower * row_j[None, :], axis=1)
        pivot = jnp.sqrt(lax.dynamic_slice_in_dim(rest, at, 1, 0)[0])
        keep = (positions >= at).astype(gram.dtype)
        pick = (positions == at).astype(gram.dtype)
        return lower + (keep * rest / pivot)[:, None] * pick[None, :]

    return lax.fori_loop(0, order, column, jnp.zeros_like(gram))


def invert_lower(lower):
    order = lower.shape[0]
    positions = jnp.arange(order, dtype=jnp.int32)

    def row_step(index, inverse):
        at = jnp.asarray(index).astype(jnp.int32)
        pick = (positions == at).astype(lower.dtype)
        row_l = lax.dynamic_slice_in_dim(lower, at, 1, 0)[0]
        pivot = lax.dynamic_slice_in_dim(row_l, at, 1, 0)[0]
        new_row = (pick - jnp.sum(row_l[:, None] * inverse, axis=0)) / pivot
        return inverse + pick[:, None] * new_row[None, :]

    return lax.fori_loop(0, order, row_step, jnp.zeros_like(lower))


def per_device(velocity, wall_metric):
    snaps = velocity.shape[0]
    planes = velocity.shape[2] - 6
    span_cells = velocity.shape[3]
    wall_cells = velocity.shape[4]
    inner = velocity[:, :, 3 : 3 + planes]
    span_padded = padded_2(inner, (("span", 3),), 3, True)
    wall_padded = padded_2(inner, (("wall", 4),), 3, False)
    du_dz = stencil(span_padded[:, 0], 2, span_cells)
    dv_dz = stencil(span_padded[:, 1], 2, span_cells)
    du_dy = wall_metric * stencil(wall_padded[:, 0], 3, wall_cells)
    dw_dy = wall_metric * stencil(wall_padded[:, 2], 3, wall_cells)
    dv_dx = stencil(velocity[:, 1], 1, planes)
    dw_dx = stencil(velocity[:, 2], 1, planes)
    vorticity = jnp.stack([dw_dy - dv_dz, du_dz - dw_dx, dv_dx - du_dy], axis=1).astype(
        jnp.bfloat16
    )
    flat = vorticity.reshape(snaps, -1)
    partial_gram = jnp.dot(flat, flat.T, preferred_element_type=jnp.float32)
    summed = lax.psum(partial_gram, ("span", "wall"))
    total_rows = (
        3 * planes * span_cells * lax.axis_size("span") * wall_cells * lax.axis_size("wall")
    )
    gram = summed / total_rows
    lower = factor_lower(gram)
    upper = lower.T
    r_inverse = invert_lower(lower).T.astype(jnp.bfloat16)
    modes = jnp.dot(r_inverse.T, flat, preferred_element_type=jnp.float32).astype(jnp.bfloat16)
    return (modes.reshape(vorticity.shape), upper)


def solution(mesh):
    in_specs = (P(None, None, None, "span", "wall"), P("wall"))
    out_specs = (P(None, None, None, "span", "wall"), P())
    return jax.shard_map(
        per_device, mesh=mesh, in_specs=in_specs, out_specs=out_specs, check_vma=False
    )
```

profile of v0, /device:TPU:0, one launch (start us, length us, event | category | flops | bytes accessed | tf_op | source)
XLA Modules:
  0.0 268.7 jit_solution(13451744703677940746)
XLA Ops:
  0.6 1.8 fusion.11
  2.4 0.8 copy.39
  3.2 2.9 %collective-permute-start.2 = (bf16[64,3,2,3,128]{4,0,3,2,1:T(8,128)(2,1)}, bf16[64,3,2,3,128]{4,0,3,2,1:T(8,128)(2,1)}, u32[]{:S(2)}, u32[]{:S(2)}) collective-permute-start(bf16[64,3,2,3,128]{4,0,3,2,1:T(8,128)(2,1)} %copy.39), channel_id=1, source_target_pairs={{0,2},{2,4},{4,6},{6,8},{8,10},{10,12},{12,14},{14,16},{16,18},{18... | collective-permute-start | bytes 884744 | tf_op jit(solution)/shard_map/ppermute | solution.py:14
  6.2 3.0 %fusion.13 = (bf16[64,3,2,8,3]{4,3,2,1,0:T(8,128)(2,1)}, bf16[64,3,2,8,3]{4,3,2,1,0:T(8,128)(2,1)}) fusion(bf16[64,3,8,8,128]{4,3,2,1,0:T(8,128)(2,1)} %param.6), kind=kLoop, calls=%fused_computation.43 | loop fusion | bytes 73728 | tf_op jit(solution)/shard_map/slice | solution.py:15
  9.1 2.4 copy.36
  11.5 2.1 collective-permute-start
  13.6 2.4 copy.38
  16.0 1.3 collective-permute-start.1
  17.3 0.8 copy.40
  18.1 4.3 %collective-permute-start.3 = (bf16[64,3,2,3,128]{4,0,3,2,1:T(8,128)(2,1)}, bf16[64,3,2,3,128]{4,0,3,2,1:T(8,128)(2,1)S(1)}, u32[]{:S(2)}, u32[]{:S(2)}) collective-permute-start(bf16[64,3,2,3,128]{4,0,3,2,1:T(8,128)(2,1)} %copy.40), channel_id=1, source_target_pairs={{2,0},{4,2},{6,4},{8,6},{10,8},{12,10},{14,12},{16,14},{18,16},{20... | collective-permute-start | bytes 884744 | tf_op jit(solution)/shard_map/ppermute | solution.py:17
  22.6 2.7 copy_bitcast_fusion
  25.3 1.3 copy.26
  26.5 1.2 copy.27
  27.8 1.0 constant_dynamic-update-slice_fusion.2
  31.4 0.7 subtract_bitcast_fusion
  34.0 40.6 %psum.7 = f32[64,64]{1,0:T(8,128)S(1)} all-reduce(f32[64,64]{1,0:T(8,128)S(1)} %convolution_bitcast_fusion), channel_id=1, replica_groups=mesh['span'=16,'wall'=2] {'span','wall'}, use_global_device_ids=true, to_apply=%region_0.0 | all-reduce | flops 4096 | bytes 32768 | tf_op jit(solution)/shard_map/psum | solution.py:81
  74.6 99.4 %while.33 = (s32[]{:T(128)}, f32[64,64]{1,0:T(8,128)S(1)}, f32[64,64]{0,1:T(8,128)S(1)}, s32[]{:T(128)}, s32[]{:T(128)}) while((s32[]{:T(128)}, f32[64,64]{1,0:T(8,128)S(1)}, f32[64,64]{0,1:T(8,128)S(1)}, s32[]{:T(128)}, s32[]{:T(128)}) %tuple.87), condition=%wide.region_3.0_spmd.clone.clone, body=%wide.region_1.0_spmd.clone.clone.sunk | while | flops 29059 | bytes 86889 | solution.py:44
  174.0 0.7 copy.34
  174.7 92.6 %while.32 = (s32[]{:T(128)}, f32[64,64]{1,0:T(8,128)S(1)}, f32[64,64]{1,0:T(8,128)S(1)}, s32[]{:T(128)}, s32[]{:T(128)}, /*index=5*/s32[]{:T(128)}) while((s32[]{:T(128)}, f32[64,64]{1,0:T(8,128)S(1)}, f32[64,64]{1,0:T(8,128)S(1)}, s32[]{:T(128)}, s32[]{:T(128)}, /*index=5*/s32[]{:T(128)}) %tuple.90), condition=%wide.region_6.0_spmd.clone, body=%wide.region_4.0_spmd.clone.sunk | while | flops 24900 | bytes 51580 | solution.py:59
  176.9 0.6 subtract_divide_fusion.2
  178.3 0.6 subtract_divide_fusion.2
  179.8 0.6 subtract_divide_fusion.2
  189.9 0.6 subtract_divide_fusion.2
  267.7 1.0 copy.44
  (922 shorter events, 146.2 us)
Async XLA Ops:
  3.2 24.5 %collective-permute-start.2 = (bf16[64,3,2,3,128]{4,0,3,2,1:T(8,128)(2,1)}, bf16[64,3,2,3,128]{4,0,3,2,1:T(8,128)(2,1)}, u32[]{:S(2)}, u32[]{:S(2)}) collective-permute-start(bf16[64,3,2,3,128]{4,0,3,2,1:T(8,128)(2,1)} %copy.39), channel_id=1, source_target_pairs={{0,2},{2,4},{4,6},{6,8},{8,10},{10,12},{12,14},{14,16},{16,18},{18... | collective-permute-start | bytes 884744 | tf_op jit(solution)/shard_map/ppermute | solution.py:14
  6.2 16.2 %copy-start = (bf16[64,3,8,8,128]{4,3,2,1,0:T(8,128)(2,1)S(1)}, bf16[64,3,8,8,128]{4,3,2,1,0:T(8,128)(2,1)}, u32[]{:S(2)}) copy-start(bf16[64,3,8,8,128]{4,3,2,1,0:T(8,128)(2,1)} %param.6) | copy-start | bytes 9437188
  11.5 13.7 %collective-permute-start = (bf16[64,3,2,8,3]{0,3,4,2,1:T(8,128)(2,1)}, bf16[64,3,2,8,3]{0,3,4,2,1:T(8,128)(2,1)}, u32[]{:S(2)}, u32[]{:S(2)}) collective-permute-start(bf16[64,3,2,8,3]{0,3,4,2,1:T(8,128)(2,1)} %copy.36), channel_id=1, source_target_pairs={{0,1},{2,3},{4,5},{6,7},{8,9},{10,11},{12,13},{14,15},{16,17},{18,... | collective-permute-start | bytes 55304 | tf_op jit(solution)/shard_map/ppermute | solution.py:14
  16.0 10.5 %collective-permute-start.1 = (bf16[64,3,2,8,3]{0,3,4,2,1:T(8,128)(2,1)}, bf16[64,3,2,8,3]{0,3,4,2,1:T(8,128)(2,1)}, u32[]{:S(2)}, u32[]{:S(2)}) collective-permute-start(bf16[64,3,2,8,3]{0,3,4,2,1:T(8,128)(2,1)} %copy.38), channel_id=1, source_target_pairs={{1,0},{3,2},{5,4},{7,6},{9,8},{11,10},{13,12},{15,14},{17,16},{19,... | collective-permute-start | bytes 55304 | tf_op jit(solution)/shard_map/ppermute | solution.py:17
  18.1 11.3 %collective-permute-start.3 = (bf16[64,3,2,3,128]{4,0,3,2,1:T(8,128)(2,1)}, bf16[64,3,2,3,128]{4,0,3,2,1:T(8,128)(2,1)S(1)}, u32[]{:S(2)}, u32[]{:S(2)}) collective-permute-start(bf16[64,3,2,3,128]{4,0,3,2,1:T(8,128)(2,1)} %copy.40), channel_id=1, source_target_pairs={{2,0},{4,2},{6,4},{8,6},{10,8},{12,10},{14,12},{16,14},{18,16},{20... | collective-permute-start | bytes 884744 | tf_op jit(solution)/shard_map/ppermute | solution.py:17
  22.5 2.7 %copy-start.3 = (f32[128]{0:T(128)S(1)}, f32[128]{0:T(128)}, u32[]{:S(2)}) copy-start(f32[128]{0:T(128)} %param.7) | copy-start | bytes 1540
  25.2 3.5 %slice-start = ((bf16[64,3,8,8,128]{4,3,2,1,0:T(8,128)(2,1)}), bf16[64,3,2,8,128]{4,3,2,1,0:T(8,128)(2,1)S(1)}, s32[]{:S(2)}) async-start(bf16[64,3,8,8,128]{4,3,2,1,0:T(8,128)(2,1)} %param.6), calls=%async_computation | async-start | bytes 1572864 | tf_op jit(solution)/shard_map/slice | solution.py:67
  30.1 1.2 copy-start.1
  31.3 1.2 copy-start.2
where the time goes:
time: 270 us; the launch traced here: 269 us
  local copies, waits for them, and re-layouts  98 us (36%)
  other arithmetic  69.6 us (26%)
  loops' own time  48.4 us (18%)
  blocking collectives  40.6 us (15%)
  starting transfers between devices  10.6 us (4%)
    another operation x1, loops' own time, factor_lower(): return lax.fori_loop(0, order, column, jnp.zeros_like(gram))  46.6 us
    div x64, other arithmetic, row_step(): new_row = (pick - jnp.sum(row_l[:, None] * inverse, axis=0)) / pivot  41.5 us
    psum x1, blocking collectives, per_device(): summed = lax.psum(partial_gram, ('span', 'wall'))  40.6 us
    dynamic_slice x64, local copies, waits for them, and re-layouts, column(): pivot = jnp.sqrt(lax.dynamic_slice_in_dim(rest, at, 1, 0)[0])  37.7 us
    dynamic_slice x64, local copies, waits for them, and re-layouts, row_step(): pivot = lax.dynamic_slice_in_dim(row_l, at, 1, 0)[0]  37.7 us
    unnamed x16, local copies, waits for them, and re-layouts  10.1 us
    reduce_sum x64, other arithmetic, column(): rest = above - jnp.sum(lower * row_j[None, :], axis=1)  6.84 us
    reduce_sum x64, other arithmetic, row_step(): new_row = (pick - jnp.sum(row_l[:, None] * inverse, axis=0)) / pivot  6.03 us
  transfers between devices with their start and end apart: 4, of which 1 were waited for; matrix products, arithmetic and copies ran while one was open for 6% of the time, Pallas kernels for 0%

commit v1 on v0

--- a/solution.py
+++ b/solution.py
@@ -78,7 +78,7 @@
     )
     flat = vorticity.reshape(snaps, -1)
     partial_gram = jnp.dot(flat, flat.T, preferred_element_type=jnp.float32)
-    summed = lax.psum(partial_gram, ("span", "wall"))
+    summed = lax.psum(lax.psum(partial_gram, "wall"), "span")
     total_rows = (
         3 * planes * span_cells * lax.axis_size("span") * wall_cells * lax.axis_size("wall")
     )

time: 270 us -> 311 us (1.15)
  blocking collectives: 40.6 us -> 81.3 us
    psum x1 -> x2, blocking collectives: 40.6 us -> 81.3 us  [per_device(): summed = lax.psum(lax.psum(partial_gram, 'wall'), 'span')]
  transfers between devices with their start and end apart: 4 -> 4, of which waited for: 1 -> 1; matrix products, arithmetic and copies ran while one was open for 6% -> 5% of each run, Pallas kernels for 0% -> 0%
where the time goes in v1:
time: 311 us; the launch traced here: 310 us
  local copies, waits for them, and re-layouts  98 us (32%)
  blocking collectives  81.3 us (26%)
  other arithmetic  69.6 us (22%)
  loops' own time  48.4 us (16%)
  starting transfers between devices  10.5 us (3%)
    psum x2, blocking collectives, per_device(): summed = lax.psum(lax.psum(partial_gram, 'wall'), 'span')  81.3 us
    another operation x1, loops' own time, factor_lower(): return lax.fori_loop(0, order, column, jnp.zeros_like(gram))  46.6 us
    div x64, other arithmetic, row_step(): new_row = (pick - jnp.sum(row_l[:, None] * inverse, axis=0)) / pivot  41.5 us
    dynamic_slice x64, local copies, waits for them, and re-layouts, column(): pivot = jnp.sqrt(lax.dynamic_slice_in_dim(rest, at, 1, 0)[0])  37.7 us
    dynamic_slice x64, local copies, waits for them, and re-layouts, row_step(): pivot = lax.dynamic_slice_in_dim(row_l, at, 1, 0)[0]  37.7 us
    unnamed x16, local copies, waits for them, and re-layouts  10.1 us
    reduce_sum x64, other arithmetic, column(): rest = above - jnp.sum(lower * row_j[None, :], axis=1)  6.87 us
  transfers between devices with their start and end apart: 4, of which 1 were waited for; matrix products, arithmetic and copies ran while one was open for 5% of the time, Pallas kernels for 0%

profile of v1, /device:TPU:0, one launch (start us, length us, event | category | flops | bytes accessed | tf_op | source)
XLA Modules:
  0.0 309.5 jit_solution(7354845102312188780)
XLA Ops:
  0.6 1.8 fusion.11
  2.4 0.8 copy.39
  3.2 2.9 collective-permute-start.2
  6.2 3.0 fusion.13
  9.1 2.4 copy.36
  11.6 2.1 collective-permute-start
  13.6 2.4 copy.38
  16.0 1.3 collective-permute-start.1
  17.3 0.8 copy.40
  18.1 4.3 %collective-permute-start.3 = (bf16[64,3,2,3,128]{4,0,3,2,1:T(8,128)(2,1)}, bf16[64,3,2,3,128]{4,0,3,2,1:T(8,128)(2,1)S(1)}, u32[]{:S(2)}, u32[]{:S(2)}) collective-permute-start(bf16[64,3,2,3,128]{4,0,3,2,1:T(8,128)(2,1)} %copy.40), channel_id=1, source_target_pairs={{2,0},{4,2},{6,4},{8,6},{10,8},{12,10},{14,12},{16,14},{18,16},{20... | collective-permute-start | bytes 884744 | tf_op jit(solution)/shard_map/ppermute | solution.py:17
  22.6 2.7 copy_bitcast_fusion
  25.3 1.3 copy.26
  26.6 1.2 copy.27
  27.8 1.0 constant_dynamic-update-slice_fusion.2
  31.4 0.7 subtract_bitcast_fusion
  34.0 4.6 %psum.14 = f32[64,64]{1,0:T(8,128)S(1)} all-reduce(f32[64,64]{1,0:T(8,128)S(1)} %convolution_bitcast_fusion), channel_id=1, replica_groups=mesh['span'=16,'wall'=2] {'wall'}, use_global_device_ids=true, to_apply=%region_0.0 | all-reduce | flops 4096 | bytes 32768 | tf_op jit(solution)/shard_map/psum | solution.py:81
  38.6 76.7 %psum.15 = f32[64,64]{1,0:T(8,128)S(1)} all-reduce(f32[64,64]{1,0:T(8,128)S(1)} %psum.14), channel_id=1, replica_groups=mesh['span'=16,'wall'=2] {'span'}, use_global_device_ids=true, to_apply=%region_1.0 | all-reduce | flops 4096 | bytes 32768 | tf_op jit(solution)/shard_map/psum | solution.py:81
  115.4 99.4 %while.33 = (s32[]{:T(128)}, f32[64,64]{1,0:T(8,128)S(1)}, f32[64,64]{0,1:T(8,128)S(1)}, s32[]{:T(128)}, s32[]{:T(128)}) while((s32[]{:T(128)}, f32[64,64]{1,0:T(8,128)S(1)}, f32[64,64]{0,1:T(8,128)S(1)}, s32[]{:T(128)}, s32[]{:T(128)}) %tuple.87), condition=%wide.region_4.0_spmd.clone.clone, body=%wide.region_2.0_spmd.clone.clone.sunk | while | flops 29059 | bytes 86889 | solution.py:44
  214.8 0.7 copy.34
  215.6 92.6 %while.32 = (s32[]{:T(128)}, f32[64,64]{1,0:T(8,128)S(1)}, f32[64,64]{1,0:T(8,128)S(1)}, s32[]{:T(128)}, s32[]{:T(128)}, /*index=5*/s32[]{:T(128)}) while((s32[]{:T(128)}, f32[64,64]{1,0:T(8,128)S(1)}, f32[64,64]{1,0:T(8,128)S(1)}, s32[]{:T(128)}, s32[]{:T(128)}, /*index=5*/s32[]{:T(128)}) %tuple.90), condition=%wide.region_7.0_spmd.clone, body=%wide.region_5.0_spmd.clone.sunk | while | flops 24900 | bytes 51580 | solution.py:59
  223.5 0.6 subtract_divide_fusion.2
  224.9 0.6 subtract_divide_fusion.2
  226.4 0.6 subtract_divide_fusion.2
  308.5 1.0 copy.44
  (923 shorter events, 146.8 us)
Async XLA Ops:
  3.2 24.6 %collective-permute-start.2 = (bf16[64,3,2,3,128]{4,0,3,2,1:T(8,128)(2,1)}, bf16[64,3,2,3,128]{4,0,3,2,1:T(8,128)(2,1)}, u32[]{:S(2)}, u32[]{:S(2)}) collective-permute-start(bf16[64,3,2,3,128]{4,0,3,2,1:T(8,128)(2,1)} %copy.39), channel_id=1, source_target_pairs={{0,2},{2,4},{4,6},{6,8},{8,10},{10,12},{12,14},{14,16},{16,18},{18... | collective-permute-start | bytes 884744 | tf_op jit(solution)/shard_map/ppermute | solution.py:14
  6.2 16.2 %copy-start = (bf16[64,3,8,8,128]{4,3,2,1,0:T(8,128)(2,1)S(1)}, bf16[64,3,8,8,128]{4,3,2,1,0:T(8,128)(2,1)}, u32[]{:S(2)}) copy-start(bf16[64,3,8,8,128]{4,3,2,1,0:T(8,128)(2,1)} %param.6) | copy-start | bytes 9437188
  11.6 13.7 %collective-permute-start = (bf16[64,3,2,8,3]{0,3,4,2,1:T(8,128)(2,1)}, bf16[64,3,2,8,3]{0,3,4,2,1:T(8,128)(2,1)}, u32[]{:S(2)}, u32[]{:S(2)}) collective-permute-start(bf16[64,3,2,8,3]{0,3,4,2,1:T(8,128)(2,1)} %copy.36), channel_id=1, source_target_pairs={{0,1},{2,3},{4,5},{6,7},{8,9},{10,11},{12,13},{14,15},{16,17},{18,... | collective-permute-start | bytes 55304 | tf_op jit(solution)/shard_map/ppermute | solution.py:14
  16.0 10.5 %collective-permute-start.1 = (bf16[64,3,2,8,3]{0,3,4,2,1:T(8,128)(2,1)}, bf16[64,3,2,8,3]{0,3,4,2,1:T(8,128)(2,1)}, u32[]{:S(2)}, u32[]{:S(2)}) collective-permute-start(bf16[64,3,2,8,3]{0,3,4,2,1:T(8,128)(2,1)} %copy.38), channel_id=1, source_target_pairs={{1,0},{3,2},{5,4},{7,6},{9,8},{11,10},{13,12},{15,14},{17,16},{19,... | collective-permute-start | bytes 55304 | tf_op jit(solution)/shard_map/ppermute | solution.py:17
  18.1 11.3 %collective-permute-start.3 = (bf16[64,3,2,3,128]{4,0,3,2,1:T(8,128)(2,1)}, bf16[64,3,2,3,128]{4,0,3,2,1:T(8,128)(2,1)S(1)}, u32[]{:S(2)}, u32[]{:S(2)}) collective-permute-start(bf16[64,3,2,3,128]{4,0,3,2,1:T(8,128)(2,1)} %copy.40), channel_id=1, source_target_pairs={{2,0},{4,2},{6,4},{8,6},{10,8},{12,10},{14,12},{16,14},{18,16},{20... | collective-permute-start | bytes 884744 | tf_op jit(solution)/shard_map/ppermute | solution.py:17
  22.6 2.7 copy-start.3
  25.3 3.5 %slice-start = ((bf16[64,3,8,8,128]{4,3,2,1,0:T(8,128)(2,1)}), bf16[64,3,2,8,128]{4,3,2,1,0:T(8,128)(2,1)S(1)}, s32[]{:S(2)}) async-start(bf16[64,3,8,8,128]{4,3,2,1,0:T(8,128)(2,1)} %param.6), calls=%async_computation | async-start | bytes 1572864 | tf_op jit(solution)/shard_map/slice | solution.py:67
  30.1 1.2 copy-start.1
  31.4 1.2 copy-start.2
